TPU v7x, 32 devices: a whole 2x2x4 slice. The times are simulated.
32 devices in a mesh: gx: 2 (over y), gy: 4 (over z), gz: 4 (over x, core).
Axes of the slice: x: 2, y: 2, z: 4, core: 2. Of those that a mesh axis runs over, the one named last changes fastest.
Arguments:
- load_cases: float32 [2, 128, 32, 256], P(None, 'gz', 'gy', 'gx'), may hold values from -6 to 6
- density_level: int32 [128, 32, 256], P('gz', 'gy', 'gx'), may hold values from 0 to 7
Outputs:
- solution: float32 [2, 128, 32, 256], P(None, 'gz', 'gy', 'gx')
All inputs are finite; a program needn't handle non-finite values.
Results may differ from a plain program's by a relative error of at most 0.00011.
Values sent between devices are 32-bit elements; how exact they have to be, the bound alone decides.
A program may use at most 192 MiB of HBM per device.

v0:
```python
import math

import jax
import jax.numpy as jnp
from jax import lax
from jax.sharding import PartitionSpec as P

LEVELS = 8


middle_point = 0.646875
half_range = 0.503125
first_weight = 1.0 / (middle_point + half_range * math.cos(math.pi / 4))
second_weight = 1.0 / (middle_point - half_range * math.cos(math.pi / 4))


def with_halo(cells, sides, width):
    for axis, dim in sides:
        count = lax.axis_size(axis)
        ends = count - 1
        head = lax.slice_in_dim(cells, 0, width, axis=dim)
        tail = lax.slice_in_dim(cells, cells.shape[dim] - width, cells.shape[dim], axis=dim)
        cells = jnp.concatenate(
            [
                lax.ppermute(tail, axis, [(i, (i + 1) % count) for i in range(ends)]),
                cells,
                lax.ppermute(head, axis, [((i + 1) % count, i) for i in range(ends)]),
            ],
            axis=dim,
        )
    return cells


def smooth_sum(padded):
    padded = 0.5 * padded[:, :-2] + padded[:, 1:-1] + 0.5 * padded[:, 2:]
    padded = 0.5 * padded[:, :, :-2] + padded[:, :, 1:-1] + 0.5 * padded[:, :, 2:]
    return 0.5 * padded[..., :-2] + padded[..., 1:-1] + 0.5 * padded[..., 2:]


def prune(values, have, want):
    cut = have - want
    if cut == 0:
        return values
    return values[
        :, cut : values.shape[1] - cut, cut : values.shape[2] - cut, cut : values.shape[3] - cut
    ]


def inside(own, halo):
    flags = []
    for axis, size in zip(("gz", "gy", "gx"), own):
        start = lax.axis_index(axis) * size
        index = start - halo + lax.iota(jnp.int32, size + 2 * halo)
        flags.append((index >= 0) & (index < size * lax.axis_size(axis)))
    return (
        flags[0][:, None, None] & flags[1][None, :, None] & flags[2][None, None, :]
    ).astype(jnp.float32)


def step(guess, scaled, weight, mask):
    centre = prune(guess, 1, 0)
    applied = (16.0 * centre - 2.0 * smooth_sum(guess)) * (1.0 / 14.0)
    return centre + weight * (scaled - mask * applied)


def restrict(values):
    return values.reshape(
        values.shape[0], values.shape[1] // 2, 2, values.shape[2] // 2, 2, values.shape[3] // 2, 2
    ).mean(axis=(2, 4, 6))


def prolong(values):
    return jnp.repeat(jnp.repeat(jnp.repeat(values, 2, axis=1), 2, axis=2), 2, axis=3)


def framed(values, width=1):
    return jnp.pad(values, ((0, 0), (width, width), (width, width), (width, width)))


def residual(target, stiffness, guess, spacing_sq):
    centre = prune(guess, 1, 0)
    return target - stiffness * (16.0 * centre - 2.0 * smooth_sum(guess)) * (1.0 / spacing_sq)


def coarse_cycle(rhs_low, stiffness_low):
    scaled_low = rhs_low * (16.0 / (14.0 * stiffness_low))
    guess_low = step(framed(first_weight * scaled_low), scaled_low, second_weight, 1.0)
    rhs_base = restrict(residual(rhs_low, stiffness_low, framed(guess_low), 16.0))
    stiffness_base = restrict(stiffness_low)
    scaled_base = rhs_base * (64.0 / (14.0 * stiffness_base))
    guess_base = step(framed(first_weight * scaled_base), scaled_base, second_weight, 1.0)
    guess_base = step(framed(guess_base), scaled_base, first_weight, 1.0)
    guess_base = step(framed(guess_base), scaled_base, second_weight, 1.0)
    guess_low = guess_low + prolong(guess_base)
    guess_low = step(framed(guess_low), scaled_low, first_weight, 1.0)
    return step(framed(guess_low), scaled_low, second_weight, 1.0)


def joined(values):
    for axis, dim in (("gx", 3), ("gy", 2), ("gz", 1)):
        values = lax.all_gather(values, axis, axis=dim, tiled=True)
    return values


SIDES = (("gx", 3), ("gy", 2), ("gz", 1))


def body(load_cases, density_level):
    stiffness_fine = (0.05 + 0.95 * (density_level.astype(jnp.float32) / (LEVELS - 1)) ** 3)[None]
    stiffness_mid = restrict(stiffness_fine)
    stiffness_low = restrict(stiffness_mid)
    own = load_cases.shape[1:]
    own_mid = tuple(size // 2 for size in own)
    own_low = tuple(size // 4 for size in own)
    scaled_fine = with_halo(load_cases * (1.0 / (14.0 * stiffness_fine)), SIDES, 3)
    mask_fine = inside(own, 2)
    guess_fine = step(
        first_weight * scaled_fine, prune(scaled_fine, 3, 2), second_weight, mask_fine
    )
    rhs_mid = restrict(residual(load_cases, stiffness_fine, prune(guess_fine, 2, 1), 1.0))
    scaled_mid = with_halo(rhs_mid * (4.0 / (14.0 * stiffness_mid)), SIDES, 4)
    mask_mid = inside(own_mid, 3)
    guess_mid = step(first_weight * scaled_mid, prune(scaled_mid, 4, 3), second_weight, mask_mid)
    rhs_low = restrict(residual(rhs_mid, stiffness_mid, prune(guess_mid, 3, 1), 4.0))
    guess_low = framed(coarse_cycle(joined(rhs_low), joined(stiffness_low)), 2)
    guess_low = lax.dynamic_slice(
        guess_low,
        (0,) + tuple(lax.axis_index(a) * n for a, n in zip(("gz", "gy", "gx"), own_low)),
        (guess_low.shape[0],) + tuple(n + 4 for n in own_low),
    )
    guess_mid = guess_mid + prune(prolong(guess_low), 4, 3)
    guess_mid = step(guess_mid, prune(scaled_mid, 4, 2), first_weight, prune(mask_mid[None], 3, 2))
    guess_mid = step(guess_mid, prune(scaled_mid, 4, 1), second_weight, prune(mask_mid[None], 3, 1))
    guess_fine = guess_fine + prolong(guess_mid)
    guess_fine = step(
        guess_fine, prune(scaled_fine, 3, 1), first_weight, prune(mask_fine[None], 2, 1)
    )
    return step(guess_fine, prune(scaled_fine, 3, 0), second_weight, 1.0)


def solution(mesh):
    in_specs = (P(None, "gz", "gy", "gx"), P("gz", "gy", "gx"))
    out_specs = P(None, "gz", "gy", "gx")
    return jax.shard_map(body, mesh=mesh, in_specs=in_specs, out_specs=out_specs, check_vma=False)
```

profile of v0, /device:TPU:0, one launch (start us, length us, event | category | flops | bytes accessed | tf_op | source)
XLA Modules:
  0.0 219.7 jit_solution(8334398188403247905)
XLA Ops:
  1.0 1.1 broadcast_multiply_fusion.2
  2.2 4.9 %collective-permute-start = (f32[2,32,8,3]{3,2,1,0:T(8,128)S(1)}, f32[2,32,8,3]{3,2,1,0:T(8,128)S(1)}, u32[]{:S(2)}, u32[]{:S(2)}) collective-permute-start(f32[2,32,8,3]{3,2,1,0:T(8,128)S(1)} %get-tuple-element.15), channel_id=1, source_target_pairs={{0,16},{1,17},{2,18},{3,19},{4,20},{5,21},{6,22},{7,23},{8,24},{9,... | collective-permute-start | bytes 18440 | tf_op jit(solution)/shard_map/ppermute | solution.py:25
  7.1 1.3 collective-permute-start.1
  8.9 9.8 %reshape_broadcast_in_dim.3 = f32[16,2,4,2,64,2]{5,4,3,2,1,0:T(8,128)} reshape(f32[32,8,128]{2,1,0:T(8,128)S(1)} %get-tuple-element.17) | data formatting | bytes 262144 | tf_op jit(solution)/shard_map/reshape;broadcast_in_dim | solution.py:67
  18.6 4.0 %reduce_sum.55 = f32[16,4,64]{2,1,0:T(4,128)S(1)} reduce(f32[16,2,4,2,64,2]{5,4,3,2,1,0:T(8,128)} %reshape_broadcast_in_dim.3, f32[]{:T(128)} %constant.57.clone.1), dimensions={1,3,5}, to_apply=%region_1.0 | reduce | flops 28672 | bytes 147460 | tf_op jit(solution)/shard_map/reduce_sum | solution.py:69
  23.3 1.1 div.83
  24.7 5.2 %all-gather = f32[8,2,64]{0,1,2:T(2,128)S(1)} all-gather(f32[8,2,32]{0,1,2:T(2,128)S(1)} %copy.174), channel_id=2, replica_groups=mesh['gx'=2,'gy'=4,'gz'=4] {'gx'}, dimensions={2}, use_global_device_ids=true | all-gather | bytes 6144 | tf_op jit(solution)/shard_map/all_gather | solution.py:101
  29.9 13.4 %all-gather.1 = f32[8,8,64]{2,0,1:T(8,128)S(1)} all-gather(f32[8,2,64]{2,0,1:T(8,128)S(1)} %copy.175), channel_id=3, replica_groups=mesh['gx'=2,'gy'=4,'gz'=4] {'gy'}, dimensions={1}, use_global_device_ids=true | all-gather | bytes 20480 | tf_op jit(solution)/shard_map/all_gather | solution.py:101
  43.3 5.4 %all-gather.2 = f32[32,8,64]{2,1,0:T(8,128)S(1)} all-gather(f32[8,8,64]{2,1,0:T(8,128)S(1)} %copy.176), channel_id=4, replica_groups=mesh['gx'=2,'gy'=4,'gz'=4] {'gz'}, dimensions={0}, use_global_device_ids=true | all-gather | bytes 81920 | tf_op jit(solution)/shard_map/all_gather | solution.py:101
  50.9 3.5 %collective-permute-start.2 = (f32[2,32,3,134]{3,2,1,0:T(4,128)S(1)}, f32[2,32,3,134]{3,2,1,0:T(4,128)S(1)}, u32[]{:S(2)}, u32[]{:S(2)}) collective-permute-start(f32[2,32,3,134]{3,2,1,0:T(4,128)S(1)} %get-tuple-element.9), channel_id=1, source_target_pairs={{0,4},{4,8},{8,12},{1,5},{5,9},{9,13},{2,6},{6,10},{10,14},{3,7},{... | collective-permute-start | bytes 308744 | tf_op jit(solution)/shard_map/ppermute | solution.py:25
  54.4 1.3 collective-permute-start.3
  56.5 4.0 %collective-permute-done.2 = f32[2,32,3,134]{3,2,1,0:T(4,128)S(1)} collective-permute-done((f32[2,32,3,134]{3,2,1,0:T(4,128)S(1)}, f32[2,32,3,134]{3,2,1,0:T(4,128)S(1)}, u32[]{:S(2)}, u32[]{:S(2)}) %collective-permute-start.2) | collective-permute-done | bytes 102944 | tf_op jit(solution)/shard_map/ppermute | solution.py:25
  60.4 4.1 %collective-permute-done.3 = f32[2,32,3,134]{3,2,1,0:T(4,128)S(1)} collective-permute-done((f32[2,32,3,134]{3,2,1,0:T(4,128)S(1)}, f32[2,32,3,134]{3,2,1,0:T(4,128)S(1)}, u32[]{:S(2)}, u32[]{:S(2)}) %collective-permute-start.3) | collective-permute-done | bytes 102944 | tf_op jit(solution)/shard_map/ppermute | solution.py:27
  64.8 1.3 collective-permute-start.4
  66.2 1.3 collective-permute-start.5
  68.3 2.8 %collective-permute-done.5 = f32[2,3,14,134]{3,0,2,1:T(2,128)S(1)} collective-permute-done((f32[2,3,14,134]{3,0,2,1:T(2,128)S(1)}, f32[2,3,14,134]{3,0,2,1:T(2,128)S(1)}, u32[]{:S(2)}, u32[]{:S(2)}) %collective-permute-start.5) | collective-permute-done | bytes 45056 | tf_op jit(solution)/shard_map/ppermute | solution.py:27
  71.1 1.5 broadcast_multiply_fusion
  73.1 1.3 fusion.6
  76.5 18.1 %reshape.211 = f32[2,16,2,4,2,64,2]{6,5,4,3,2,1,0:T(8,128)} reshape(f32[2,32,8,128]{3,2,1,0:T(8,128)S(1)} %fusion.90) | data formatting | bytes 524288 | tf_op jit(solution)/shard_map/reshape | solution.py:67
  94.7 7.0 %reduce_sum.54 = f32[2,16,4,64]{3,2,1,0:T(4,128)S(1)} reduce(f32[2,16,2,4,2,64,2]{6,5,4,3,2,1,0:T(8,128)} %reshape.211, f32[]{:T(128)} %constant.57.clone.1), dimensions={2,4,6}, to_apply=%region_0.0 | reduce | flops 57344 | bytes 294916 | tf_op jit(solution)/shard_map/reduce_sum | solution.py:69
  101.8 3.9 %collective-permute-start.6 = (f32[2,16,4,4]{3,2,1,0:T(4,128)S(1)}, f32[2,16,4,4]{3,2,1,0:T(4,128)S(1)}, u32[]{:S(2)}, u32[]{:S(2)}) collective-permute-start(f32[2,16,4,4]{3,2,1,0:T(4,128)S(1)} %get-tuple-element.19), channel_id=1, source_target_pairs={{0,16},{1,17},{2,18},{3,19},{4,20},{5,21},{6,22},{7,23},{8,24},{9,... | collective-permute-start | bytes 6152 | tf_op jit(solution)/shard_map/ppermute | solution.py:25
  105.8 1.3 collective-permute-start.7
  107.8 4.1 %collective-permute-done.7 = f32[2,16,4,4]{3,2,1,0:T(4,128)S(1)} collective-permute-done((f32[2,16,4,4]{3,2,1,0:T(4,128)S(1)}, f32[2,16,4,4]{3,2,1,0:T(4,128)S(1)}, u32[]{:S(2)}, u32[]{:S(2)}) %collective-permute-start.7) | collective-permute-done | bytes 2080 | tf_op jit(solution)/shard_map/ppermute | solution.py:27
  112.1 3.1 %collective-permute-start.8 = (f32[2,16,4,72]{3,1,2,0:T(8,128)S(1)}, f32[2,16,4,72]{3,1,2,0:T(8,128)S(1)}, u32[]{:S(2)}, u32[]{:S(2)}) collective-permute-start(f32[2,16,4,72]{3,1,2,0:T(8,128)S(1)} %pad_maximum_fusion.8), channel_id=1, source_target_pairs={{0,4},{4,8},{8,12},{1,5},{5,9},{9,13},{2,6},{6,10},{10,14},{3,7},{... | collective-permute-start | bytes 110600 | tf_op jit(solution)/shard_map/ppermute | solution.py:25
  115.2 1.5 collective-permute-start.9
  117.4 5.6 %reshape.214 = f32[16,2,4,2,32,2]{5,4,3,2,1,0:T(8,128)} reshape(f32[32,8,64]{2,1,0:T(8,128)S(1)} %copy-done.12) | data formatting | bytes 131072 | tf_op jit(solution)/shard_map/reshape | solution.py:67
  123.0 2.6 %reduce_sum.59 = f32[16,4,32]{2,1,0:T(4,128)S(1)} reduce(f32[16,2,4,2,32,2]{5,4,3,2,1,0:T(8,128)} %reshape.214, f32[]{:T(128)} %constant.57.clone.1), dimensions={1,3,5}, to_apply=%region_5.6 | reduce | flops 14336 | bytes 73732 | tf_op jit(solution)/shard_map/reduce_sum | solution.py:69
  126.3 3.3 %collective-permute-start.10 = (f32[2,4,12,72]{3,1,2,0:T(4,128)}, f32[2,4,12,72]{3,1,2,0:T(4,128)S(1)}, u32[]{:S(2)}, u32[]{:S(2)}) collective-permute-start(f32[2,4,12,72]{3,1,2,0:T(4,128)} %get-tuple-element.11), channel_id=1, source_target_pairs={{0,1},{1,2},{2,3},{4,5},{5,6},{6,7},{8,9},{9,10},{10,11},{12,13},{... | collective-permute-start | bytes 82952 | tf_op jit(solution)/shard_map/ppermute | solution.py:25
  129.7 1.3 collective-permute-start.11
  132.6 1.3 collective-permute-done.11
  136.6 3.5 %reshape.212 = f32[2,8,2,2,2,32,2]{6,5,2,1,4,3,0:T(8,128)} reshape(f32[2,16,4,64]{3,1,2,0:T(8,128)S(1)} %copy.169) | data formatting | bytes 65536 | tf_op jit(solution)/shard_map/reshape | solution.py:67
  140.1 1.8 reduce_sum.56
  142.1 4.9 %all_gather.18 = f32[2,8,2,64]{1,2,0,3:T(2,128)S(1)} all-gather(f32[2,8,2,32]{1,2,0,3:T(2,128)S(1)} %copy.170), channel_id=1, replica_groups=mesh['gx'=2,'gy'=4,'gz'=4] {'gx'}, dimensions={3}, use_global_device_ids=true | all-gather | bytes 12288 | tf_op jit(solution)/shard_map/all_gather | solution.py:101
  147.1 14.6 %all_gather.19 = f32[2,8,8,64]{3,1,0,2:T(8,128)S(1)} all-gather(f32[2,8,2,64]{3,1,0,2:T(8,128)S(1)} %copy.171), channel_id=1, replica_groups=mesh['gx'=2,'gy'=4,'gz'=4] {'gy'}, dimensions={2}, use_global_device_ids=true | all-gather | bytes 40960 | tf_op jit(solution)/shard_map/all_gather | solution.py:101
  161.7 6.9 %all_gather.20 = f32[2,32,8,64]{3,2,0,1:T(8,128)S(1)} all-gather(f32[2,8,8,64]{3,2,0,1:T(8,128)S(1)} %copy.172), channel_id=1, replica_groups=mesh['gx'=2,'gy'=4,'gz'=4] {'gz'}, dimensions={1}, use_global_device_ids=true | all-gather | bytes 163840 | tf_op jit(solution)/shard_map/all_gather | solution.py:101
  172.3 1.0 fusion.60
  173.3 1.9 copy.181
  175.2 10.9 %reshape.213 = f32[2,16,2,4,2,32,2]{6,5,4,3,2,1,0:T(8,128)} reshape(f32[2,32,8,64]{3,2,1,0:T(8,128)} %copy.181) | data formatting | bytes 262144 | tf_op jit(solution)/shard_map/reshape | solution.py:67
  186.1 4.1 %reduce_sum.58 = f32[2,16,4,32]{3,2,1,0:T(4,128)S(1)} reduce(f32[2,16,2,4,2,32,2]{6,5,4,3,2,1,0:T(8,128)} %reshape.213, f32[]{:T(128)} %constant.57.clone.1), dimensions={2,4,6}, to_apply=%region_4.5 | reduce | flops 28672 | bytes 147460 | tf_op jit(solution)/shard_map/reduce_sum | solution.py:69
  193.6 1.7 copy.183
  195.3 1.0 broadcast_in_dim.19
  200.2 1.1 slice.756
  201.4 1.6 copy.192
  205.4 1.3 copy.190
  206.6 2.8 %broadcast_in_dim.47 = f32[2,36,12,66,2]{1,0,4,3,2:T(2,128)} broadcast(f32[2,36,12,66]{1,0,3,2:T(2,128)} %copy.190), dimensions={0,1,2,3} | broadcast | bytes 684288 | tf_op jit(solution)/shard_map/broadcast_in_dim | solution.py:73
  209.4 4.2 %copy.191 = f32[2,36,12,132]{3,2,1,0:T(8,128)} copy(f32[2,36,12,132]{1,0,3,2:T(2,128)} %bitcast.28) | data formatting | bytes 912384 | tf_op jit(solution)/shard_map/reshape | solution.py:73
  213.6 1.5 add.519
  216.3 1.3 fusion.15
  (170 shorter events, 32.3 us)
Async XLA Ops:
  1.0 1.2 copy-start.15
  1.0 7.9 %copy-start.13 = (f32[32,8,128]{2,1,0:T(8,128)}, f32[32,8,128]{2,1,0:T(8,128)S(1)}, u32[]{:S(2)}) copy-start(f32[32,8,128]{2,1,0:T(8,128)S(1)} %get-tuple-element.17) | copy-start | bytes 393220
  2.2 48.3 %collective-permute-start = (f32[2,32,8,3]{3,2,1,0:T(8,128)S(1)}, f32[2,32,8,3]{3,2,1,0:T(8,128)S(1)}, u32[]{:S(2)}, u32[]{:S(2)}) collective-permute-start(f32[2,32,8,3]{3,2,1,0:T(8,128)S(1)} %get-tuple-element.15), channel_id=1, source_target_pairs={{0,16},{1,17},{2,18},{3,19},{4,20},{5,21},{6,22},{7,23},{8,24},{9,... | collective-permute-start | bytes 18440 | tf_op jit(solution)/shard_map/ppermute | solution.py:25
  7.1 43.4 %collective-permute-start.1 = (f32[2,32,8,3]{3,2,1,0:T(8,128)S(1)}, f32[2,32,8,3]{3,2,1,0:T(8,128)S(1)}, u32[]{:S(2)}, u32[]{:S(2)}) collective-permute-start(f32[2,32,8,3]{3,2,1,0:T(8,128)S(1)} %get-tuple-element.16), channel_id=1, source_target_pairs={{16,0},{17,1},{18,2},{19,3},{20,4},{21,5},{22,6},{23,7},{24,8},{25... | collective-permute-start | bytes 18440 | tf_op jit(solution)/shard_map/ppermute | solution.py:27
  23.3 1.3 copy-start.23
  48.7 2.2 copy-start.11
  50.5 14.1 %copy-start.9 = (f32[2,32,8,3]{3,2,1,0:T(8,128)}, f32[2,32,8,3]{3,2,1,0:T(8,128)S(1)}, u32[]{:S(2)}) copy-start(f32[2,32,8,3]{3,2,1,0:T(8,128)S(1)} %collective-permute-done.1) | copy-start | bytes 18436
  50.9 9.5 %collective-permute-start.2 = (f32[2,32,3,134]{3,2,1,0:T(4,128)S(1)}, f32[2,32,3,134]{3,2,1,0:T(4,128)S(1)}, u32[]{:S(2)}, u32[]{:S(2)}) collective-permute-start(f32[2,32,3,134]{3,2,1,0:T(4,128)S(1)} %get-tuple-element.9), channel_id=1, source_target_pairs={{0,4},{4,8},{8,12},{1,5},{5,9},{9,13},{2,6},{6,10},{10,14},{3,7},{... | collective-permute-start | bytes 308744 | tf_op jit(solution)/shard_map/ppermute | solution.py:25
  54.4 10.2 %collective-permute-start.3 = (f32[2,32,3,134]{3,2,1,0:T(4,128)S(1)}, f32[2,32,3,134]{3,2,1,0:T(4,128)S(1)}, u32[]{:S(2)}, u32[]{:S(2)}) collective-permute-start(f32[2,32,3,134]{3,2,1,0:T(4,128)S(1)} %get-tuple-element.10), channel_id=1, source_target_pairs={{4,0},{8,4},{12,8},{5,1},{9,5},{13,9},{6,2},{10,6},{14,10},{7,3},{... | collective-permute-start | bytes 308744 | tf_op jit(solution)/shard_map/ppermute | solution.py:27
  64.8 3.5 %collective-permute-start.4 = (f32[2,3,14,134]{3,0,2,1:T(2,128)S(1)}, f32[2,3,14,134]{3,0,2,1:T(2,128)S(1)}, u32[]{:S(2)}, u32[]{:S(2)}) collective-permute-start(f32[2,3,14,134]{3,0,2,1:T(2,128)S(1)} %copy.160), channel_id=1, source_target_pairs={{0,1},{1,2},{2,3},{4,5},{5,6},{6,7},{8,9},{9,10},{10,11},{12,13},{... | collective-permute-start | bytes 135080 | tf_op jit(solution)/shard_map/ppermute | solution.py:25
  66.2 4.9 %collective-permute-start.5 = (f32[2,3,14,134]{3,0,2,1:T(2,128)S(1)}, f32[2,3,14,134]{3,0,2,1:T(2,128)S(1)}, u32[]{:S(2)}, u32[]{:S(2)}) collective-permute-start(f32[2,3,14,134]{3,0,2,1:T(2,128)S(1)} %copy.161), channel_id=1, source_target_pairs={{1,0},{2,1},{3,2},{5,4},{6,5},{7,6},{9,8},{10,9},{11,10},{13,12},{... | collective-permute-start | bytes 135080 | tf_op jit(solution)/shard_map/ppermute | solution.py:27
  75.3 1.0 copy-start.7
  75.3 1.0 copy-start.14
  94.6 7.1 %copy-start.26 = (f32[16,4,64]{2,1,0:T(4,128)S(1)}, f32[16,4,64]{2,1,0:T(4,128)}, u32[]{:S(2)}) copy-start(f32[16,4,64]{2,1,0:T(4,128)} %get-tuple-element.22) | copy-start | bytes 49156
  94.6 12.4 %copy-start.20 = (f32[1,22,10,70]{3,2,1,0:T(8,128)S(1)}, f32[1,22,10,70]{3,2,1,0:T(8,128)}, u32[]{:S(2)}) copy-start(f32[1,22,10,70]{3,2,1,0:T(8,128)} %and_convert_fusion) | copy-start | bytes 184804
  101.7 15.7 %copy-start.12 = (f32[32,8,64]{2,1,0:T(8,128)S(1)}, f32[32,8,64]{2,1,0:T(8,128)}, u32[]{:S(2)}) copy-start(f32[32,8,64]{2,1,0:T(8,128)} %copy-done.11) | copy-start | bytes 196612
  101.8 6.0 %collective-permute-start.6 = (f32[2,16,4,4]{3,2,1,0:T(4,128)S(1)}, f32[2,16,4,4]{3,2,1,0:T(4,128)S(1)}, u32[]{:S(2)}, u32[]{:S(2)}) collective-permute-start(f32[2,16,4,4]{3,2,1,0:T(4,128)S(1)} %get-tuple-element.19), channel_id=1, source_target_pairs={{0,16},{1,17},{2,18},{3,19},{4,20},{5,21},{6,22},{7,23},{8,24},{9,... | collective-permute-start | bytes 6152 | tf_op jit(solution)/shard_map/ppermute | solution.py:25
  105.8 6.2 %collective-permute-start.7 = (f32[2,16,4,4]{3,2,1,0:T(4,128)S(1)}, f32[2,16,4,4]{3,2,1,0:T(4,128)S(1)}, u32[]{:S(2)}, u32[]{:S(2)}) collective-permute-start(f32[2,16,4,4]{3,2,1,0:T(4,128)S(1)} %get-tuple-element.20), channel_id=1, source_target_pairs={{16,0},{17,1},{18,2},{19,3},{20,4},{21,5},{22,6},{23,7},{24,8},{25... | collective-permute-start | bytes 6152 | tf_op jit(solution)/shard_map/ppermute | solution.py:27
  112.1 13.5 %collective-permute-start.8 = (f32[2,16,4,72]{3,1,2,0:T(8,128)S(1)}, f32[2,16,4,72]{3,1,2,0:T(8,128)S(1)}, u32[]{:S(2)}, u32[]{:S(2)}) collective-permute-start(f32[2,16,4,72]{3,1,2,0:T(8,128)S(1)} %pad_maximum_fusion.8), channel_id=1, source_target_pairs={{0,4},{4,8},{8,12},{1,5},{5,9},{9,13},{2,6},{6,10},{10,14},{3,7},{... | collective-permute-start | bytes 110600 | tf_op jit(solution)/shard_map/ppermute | solution.py:25
  115.2 10.4 %collective-permute-start.9 = (f32[2,16,4,72]{3,1,2,0:T(8,128)S(1)}, f32[2,16,4,72]{3,1,2,0:T(8,128)S(1)}, u32[]{:S(2)}, u32[]{:S(2)}) collective-permute-start(f32[2,16,4,72]{3,1,2,0:T(8,128)S(1)} %pad_maximum_fusion.8), channel_id=1, source_target_pairs={{4,0},{8,4},{12,8},{5,1},{9,5},{13,9},{6,2},{10,6},{14,10},{7,3},{... | collective-permute-start | bytes 110600 | tf_op jit(solution)/shard_map/ppermute | solution.py:27
  123.0 9.4 %copy-start.21 = (f32[32,8,64]{2,1,0:T(8,128)S(1)}, f32[32,8,64]{2,1,0:T(8,128)}, u32[]{:S(2)}) copy-start(f32[32,8,64]{2,1,0:T(8,128)} %multiply_divide_fusion) | copy-start | bytes 196612
  126.3 6.3 %collective-permute-start.10 = (f32[2,4,12,72]{3,1,2,0:T(4,128)}, f32[2,4,12,72]{3,1,2,0:T(4,128)S(1)}, u32[]{:S(2)}, u32[]{:S(2)}) collective-permute-start(f32[2,4,12,72]{3,1,2,0:T(4,128)} %get-tuple-element.11), channel_id=1, source_target_pairs={{0,1},{1,2},{2,3},{4,5},{5,6},{6,7},{8,9},{9,10},{10,11},{12,13},{... | collective-permute-start | bytes 82952 | tf_op jit(solution)/shard_map/ppermute | solution.py:25
  129.7 4.3 %collective-permute-start.11 = (f32[2,4,12,72]{3,1,2,0:T(4,128)S(1)}, f32[2,4,12,72]{3,1,2,0:T(4,128)S(1)}, u32[]{:S(2)}, u32[]{:S(2)}) collective-permute-start(f32[2,4,12,72]{3,1,2,0:T(4,128)S(1)} %get-tuple-element.12), channel_id=1, source_target_pairs={{1,0},{2,1},{3,2},{5,4},{6,5},{7,6},{9,8},{10,9},{11,10},{13,12},{... | collective-permute-start | bytes 82952 | tf_op jit(solution)/shard_map/ppermute | solution.py:27
  132.6 36.3 %copy-start = (f32[32,8,64]{0,1,2:T(8,128)}, f32[32,8,64]{0,1,2:T(8,128)S(1)}, u32[]{:S(2)}) copy-start(f32[32,8,64]{0,1,2:T(8,128)S(1)} %copy.177) | copy-start | bytes 196612
  134.2 0.8 copy-start.5
  134.2 1.1 copy-start.19
  135.2 1.2 copy-start.24
  135.7 0.8 copy-start.3
  169.6 1.0 copy-start.1
  171.3 1.0 copy-start.17
  190.2 2.2 %copy-start.18 = (f32[16,4,32]{2,1,0:T(4,128)S(1)}, f32[16,4,32]{2,1,0:T(4,128)}, u32[]{:S(2)}) copy-start(f32[16,4,32]{2,1,0:T(4,128)} %divide_multiply_fusion) | copy-start | bytes 24580
  197.0 1.0 copy-start.2
  200.2 2.7 %copy-start.4 = (f32[2,22,10,70]{3,2,1,0:T(8,128)S(1)}, f32[2,22,10,70]{3,2,1,0:T(8,128)}, u32[]{:S(2)}) copy-start(f32[2,22,10,70]{3,2,1,0:T(8,128)} %copy-done.3) | copy-start | bytes 369604
  203.0 1.0 copy-start.6
  203.0 1.0 copy-start.22
  204.0 0.9 copy-start.25
  215.3 1.1 copy-start.10
  217.7 1.0 copy-start.8
  217.8 1.0 copy-start.16
where the time goes:
time: 221 us; the launch traced here: 220 us
  local copies, waits for them, and re-layouts  76.5 us (35%)
  blocking collectives  50.4 us (23%)
  other arithmetic  47.5 us (21%)
  starting transfers between devices  28 us (13%)
  waiting for transfers between devices  16.3 us (7%)
    all_gather x6, blocking collectives, joined(): values = lax.all_gather(values, axis, axis=dim, tiled=True)  50.4 us
    reshape x4, local copies, waits for them, and re-layouts, restrict(): values.reshape(values.shape[0], values.shape[1] // 2, 2, values.shape[2]...  38.1 us
    ppermute x6, starting transfers between devices, with_halo(): lax.ppermute(tail, axis, [(i, (i + 1) % count) for i in range(ends)])  20.1 us
    reduce_sum x6, other arithmetic, restrict(): return values.reshape(values.shape[0], values.shape[1] // 2, 2, values.sh...  19.7 us
    ppermute x6, waiting for transfers between devices, with_halo(): lax.ppermute(head, axis, [((i + 1) % count, i) for i in range(ends)])  12.3 us
    another operation x1, local copies, waits for them, and re-layouts, restrict(): values.reshape(values.shape[0], values.shape[1] // 2, 2, values.shape[2]...  9.77 us
    unnamed x55, local copies, waits for them, and re-layouts  9.29 us
    ppermute x6, starting transfers between devices, with_halo(): lax.ppermute(head, axis, [((i + 1) % count, i) for i in range(ends)])  7.93 us
  transfers between devices with their start and end apart: 12, of which 5 were waited for; matrix products, arithmetic and copies ran while one was open for 14% of the time, Pallas kernels for 0%

commit v1 on v0

--- a/solution.py
+++ b/solution.py
@@ -3,6 +3,8 @@
 import jax
 import jax.numpy as jnp
 from jax import lax
+from jax.experimental import pallas as pl
+from jax.experimental.pallas import tpu as pltpu
 from jax.sharding import PartitionSpec as P
 
 LEVELS = 8
@@ -138,7 +140,260 @@
     return step(guess_fine, prune(scaled_fine, 3, 0), second_weight, 1.0)
 
 
+HIGHEST = lax.Precision.HIGHEST
+
+
+def dot(a, b):
+    return jnp.dot(a, b, precision=HIGHEST, preferred_element_type=jnp.float32)
+
+
+def iota(shape, dim):
+    return lax.broadcasted_iota(jnp.int32, shape, dim)
+
+
+def pick(condition):
+    return jnp.where(condition, 1.0, 0.0).astype(jnp.float32)
+
+
+def blur(u, close_z=False):
+    rows, depth, length = u.shape
+    v = u[1:-1] + 0.5 * (u[:-2] + u[2:])
+    down, up = pltpu.roll(v, 1, 1), pltpu.roll(v, depth - 1, 1)
+    if close_z:
+        z = iota((1, depth, length), 1)
+        down, up = down * pick(z > 0), up * pick(z < depth - 1)
+    v = v + 0.5 * (down + up)
+    x = iota((1, 1, length), 2)
+    down, up = pltpu.roll(v, 1, 2) * pick(x > 0), pltpu.roll(v, length - 1, 2) * pick(x < length - 1)
+    return v + 0.5 * (down + up)
+
+
+def move(guess, scaled, weight, mask):
+    applied = (16.0 / 14.0) * guess[1:-1] - (2.0 / 14.0) * blur(guess)
+    return (guess[1:-1] + weight * (scaled - applied)) * mask
+
+
+def move_whole(guess, scaled, weight, mask):
+    edge = jnp.zeros((1,) + guess.shape[1:], jnp.float32)
+    total = blur(jnp.concatenate([edge, guess, edge], 0), True)
+    return (guess + weight * (scaled - ((16.0 / 14.0) * guess - (2.0 / 14.0) * total))) * mask
+
+
+def halve(values, length_out, first=0):
+    rows, depth, length = values.shape
+    values = values.reshape(rows // 2, 2, depth, length)
+    values = values[:, 0] + values[:, 1]
+    pairs = (rows // 2) * depth
+    across = pick(iota((length, length_out), 0) // 2 + first == iota((length, length_out), 1)) * 0.125
+    along = pick(iota((pairs // 2, pairs), 1) // 2 == iota((pairs // 2, pairs), 0))
+    flat = dot(along, dot(values.reshape(pairs, length), across))
+    return flat.reshape(rows // 2, depth // 2, length_out)
+
+
+def double(values, depth_out, offset, length_out):
+    rows, depth, length = values.shape
+    across = pick(iota((length, length_out), 1) // 2 == iota((length, length_out), 0))
+    along = pick(iota((depth_out, depth), 0) // 2 + offset == iota((depth_out, depth), 1))
+    wide = dot(values.reshape(rows * depth, length), across).reshape(rows, depth, length_out)
+    tall = [dot(along, wide[row]) for row in range(rows)]
+    return jnp.stack([tall[row // 2] for row in range(2 * rows)], 0)
+
+
+def domain(rows, depth, length, halo_y, halo_z, own_y, own_z, me_y, me_z, ny, nz):
+    y = iota((rows, 1, length), 0) + (me_y * own_y - halo_y)
+    z = iota((1, depth, length), 1) + (me_z * own_z - halo_z)
+    return pick((y >= 0) & (y < own_y * ny)) * pick((z >= 0) & (z < own_z * nz))
+
+
+SHIFTS = tuple((dy, dz) for dy in (-1, 0, 1) for dz in (-1, 0, 1))
+
+
+def kernel(ny, nz, g_ref, b_ref, s_ref, out_ref, gbuf, bbuf, sbuf, mbuf, lbuf, wide, obuf, rbuf,
+           send_a, recv_a, send_b, recv_b, send_c, recv_c, send_d, recv_d):
+    c, my, mz = lax.axis_index("gx"), lax.axis_index("gy"), lax.axis_index("gz")
+    other = 1 - c
+    oy, oz, ox = s_ref.shape
+
+    def at(k, y, z):
+        return {"gx": k, "gy": y, "gz": z}
+
+    def near(dy, dz):
+        return lax.rem(my + dy + ny, ny), lax.rem(mz + dz + nz, nz)
+
+    def group(step):
+        index = lax.rem(my * nz + mz + step, ny * nz)
+        return index // nz, lax.rem(index, nz)
+
+    barrier = pltpu.get_barrier_semaphore()
+    for step in range(1, ny * nz):
+        pl.semaphore_signal(barrier, 1, device_id=at(c, *group(step)), device_id_type=pl.DeviceIdType.MESH)
+    for shift in SHIFTS:
+        pl.semaphore_signal(barrier, 1, device_id=at(other, *near(*shift)), device_id_type=pl.DeviceIdType.MESH)
+    gbuf[c, 3 : 3 + oy, 8 : 8 + oz, :] = g_ref[c]
+    bbuf[c] = b_ref[c]
+    sbuf[c] = s_ref[...]
+    pl.semaphore_wait(barrier, ny * nz - 1 + 9)
+
+    def remote(src, dst, sends, recvs, slot, device):
+        copy = pltpu.make_async_remote_copy(
+            src_ref=src, dst_ref=dst, send_sem=sends.at[slot], recv_sem=recvs.at[slot],
+            device_id=device, device_id_type=pl.DeviceIdType.MESH,
+        )
+        copy.start()
+        return copy
+
+    def cut(shift, own, reach, room):
+        if shift == 0:
+            return 0, room, own
+        return (own - reach, room - reach, reach) if shift > 0 else (0, room + own, reach)
+
+    phase = []
+    slot = 0
+    for k, who in ((0, other), (1, c)):
+        for dy, dz in SHIFTS:
+            if k == 1 and (dy, dz) == (0, 0):
+                continue
+            fy, ty, ly = cut(dy, oy, 3, 3)
+            fz, tz, lz = cut(dz, oz, 8, 8)
+            phase.append(remote(
+                g_ref.at[who, fy : fy + ly, fz : fz + lz, :],
+                gbuf.at[c, ty : ty + ly, tz : tz + lz, :],
+                send_a, recv_a, slot, at(who, *near(dy, dz)),
+            ))
+            slot += 1
+    phase.append(remote(b_ref.at[other], bbuf.at[c], send_a, recv_a, slot, at(other, my, mz)))
+    phase.append(remote(s_ref, sbuf.at[c], send_a, recv_a, slot + 1, at(other, my, mz)))
+    for copy in phase:
+        copy.wait()
+
+    length = 2 * ox
+    depth = oz + 16
+    fine = (depth, length, )
+    def mask_fine(halo):
+        return domain(oy + 2 * halo, depth, length, halo, 8, oy, oz, my, mz, ny, nz)
+    scaled = jnp.concatenate([gbuf[0], gbuf[1]], -1) * mask_fine(3)
+    target = jnp.concatenate([bbuf[0], bbuf[1]], -1)
+    stiff = jnp.concatenate([sbuf[0], sbuf[1]], -1)
+    guess = move(first_weight * scaled, scaled[1:-1], second_weight, mask_fine(2))
+    applied = 16.0 * guess[2:-2] - 2.0 * blur(guess[1:-1])
+    rhs_mid = halve(target - stiff * applied[:, 8 : 8 + oz], ox)
+    stiff_mid = halve(stiff, ox)
+
+    hy, hz = oy // 2, oz // 2
+    mbuf[4 : 4 + hy, 8 : 8 + hz, :] = rhs_mid * (4.0 / (14.0 * stiff_mid))
+    phase = []
+    for slot, (dy, dz) in enumerate(shift for shift in SHIFTS if shift != (0, 0)):
+        fy, ty, ly = cut(dy, hy, 4, 4)
+        fz, tz, lz = cut(dz, hz, 8, 8)
+        phase.append(remote(
+            mbuf.at[4 + fy : 4 + fy + ly, 8 + fz : 8 + fz + lz, :],
+            mbuf.at[ty : ty + ly, tz : tz + lz, :],
+            send_b, recv_b, slot, at(c, *near(dy, dz)),
+        ))
+    packed_stiff = halve(stiff_mid, ox, ox // 2)
+    for copy in phase:
+        copy.wait()
+
+    def mask_mid(halo):
+        return domain(hy + 2 * halo, hz + 16, ox, halo, 8, hy, hz, my, mz, ny, nz)
+    scaled_mid = mbuf[...] * mask_mid(4)
+    guess_mid = move(first_weight * scaled_mid, scaled_mid[1:-1], second_weight, mask_mid(3))
+    applied = 16.0 * guess_mid[3:-3] - 2.0 * blur(guess_mid[2:-2])
+    residue = rhs_mid - stiff_mid * applied[:, 8 : 8 + hz] * 0.25
+
+    qy, qz = oy // 4, oz // 4
+    lbuf[mz, my] = halve(residue, ox) + packed_stiff
+    phase = []
+    for step in range(1, ny * nz):
+        phase.append(remote(
+            lbuf.at[mz, my], lbuf.at[mz, my], send_c, recv_c, step - 1, at(c, *group(step))
+        ))
+    for copy in phase:
+        copy.wait()
+    packed = jnp.concatenate(
+        [jnp.concatenate([lbuf[z, y] for y in range(ny)], 0) for z in range(nz)], 1
+    )
+    x = iota((1, 1, ox), 2)
+    mask_low, mask_base = pick(x < ox // 2), pick(x < ox // 4)
+    rhs_low = packed * mask_low
+    stiff_low = pltpu.roll(packed, ox // 2, 2) * mask_low + (1.0 - mask_low)
+    scaled_low = rhs_low * (16.0 / (14.0 * stiff_low))
+    guess_low = move_whole(first_weight * scaled_low, scaled_low, second_weight, mask_low)
+    edge = jnp.zeros((1,) + guess_low.shape[1:], jnp.float32)
+    applied = 16.0 * guess_low - 2.0 * blur(jnp.concatenate([edge, guess_low, edge], 0), True)
+    rhs_base = halve((rhs_low - stiff_low * applied * 0.0625) * mask_low, ox)
+    stiff_base = halve(stiff_low, ox) * mask_base + (1.0 - mask_base)
+    scaled_base = rhs_base * (64.0 / (14.0 * stiff_base))
+    guess_base = move_whole(first_weight * scaled_base, scaled_base, second_weight, mask_base)
+    guess_base = move_whole(guess_base, scaled_base, first_weight, mask_base)
+    guess_base = move_whole(guess_base, scaled_base, second_weight, mask_base)
+    guess_low = guess_low + double(guess_base, qz * nz, 0, ox)
+    guess_low = move_whole(guess_low, scaled_low, first_weight, mask_low)
+    guess_low = move_whole(guess_low, scaled_low, second_weight, mask_low)
+
+    wide[...] = jnp.zeros(wide.shape, jnp.float32)
+    wide[2 : 2 + qy * ny, 8 : 8 + qz * nz, :] = guess_low
+    around = wide[pl.ds(my * qy, qy + 4), pl.ds(pl.multiple_of(mz * qz, 8), qz + 16), :]
+    guess_mid = guess_mid + double(around, hz + 16, 4, ox)[1:-1]
+    guess_mid = move(guess_mid, scaled_mid[2:-2], first_weight, mask_mid(2))
+    guess_mid = move(guess_mid, scaled_mid[3:-3], second_weight, mask_mid(1))
+    guess = guess + double(guess_mid, depth, 4, length)
+    guess = move(guess, scaled[2:-2], first_weight, mask_fine(1))
+    guess = move(guess, scaled[3:-3], second_weight, 1.0)[:, 8 : 8 + oz]
+
+    obuf[0] = guess[:, :, :ox]
+    obuf[1] = guess[:, :, ox:]
+    copy = remote(obuf.at[other], rbuf, send_d, recv_d, 0, at(other, my, mz))
+    out_ref[c] = obuf[c]
+    copy.wait()
+    out_ref[other] = rbuf[...]
+
+
+def split_cases(ny, nz, load_cases, density_level):
+    stiffness = (0.05 + 0.95 * (density_level.astype(jnp.float32) / (LEVELS - 1)) ** 3)
+    stiffness = stiffness.transpose(1, 0, 2)
+    target = load_cases.transpose(0, 2, 1, 3)
+    scaled = target * (1.0 / (14.0 * stiffness))
+    oy, oz, ox = stiffness.shape
+    f32 = jnp.float32
+    spec = pl.BlockSpec(memory_space=pltpu.VMEM)
+    dma = pltpu.SemaphoreType.DMA
+    many = ny * nz - 1
+    out = pl.pallas_call(
+        lambda *refs: kernel(ny, nz, *refs),
+        out_shape=jax.ShapeDtypeStruct(target.shape, f32),
+        in_specs=[spec] * 3,
+        out_specs=spec,
+        scratch_shapes=[
+            pltpu.VMEM((2, oy + 6, oz + 16, ox), f32),
+            pltpu.VMEM((2, oy, oz, ox), f32),
+            pltpu.VMEM((2, oy, oz, ox), f32),
+            pltpu.VMEM((oy // 2 + 8, oz // 2 + 16, ox), f32),
+            pltpu.VMEM((nz, ny, oy // 4, oz // 4, ox), f32),
+            pltpu.VMEM((oy // 4 * ny + 4, oz // 4 * nz + 16, ox), f32),
+            pltpu.VMEM((2, oy, oz, ox), f32),
+            pltpu.VMEM((oy, oz, ox), f32),
+            dma((19,)), dma((19,)), dma((8,)), dma((8,)), dma((many,)), dma((many,)),
+            dma((1,)), dma((1,)),
+        ],
+        compiler_params=pltpu.CompilerParams(
+            collective_id=0, has_side_effects=True, vmem_limit_bytes=60 * 2**20
+        ),
+    )(scaled, target, stiffness)
+    return out.transpose(0, 2, 1, 3)
+
+
 def solution(mesh):
     in_specs = (P(None, "gz", "gy", "gx"), P("gz", "gy", "gx"))
     out_specs = P(None, "gz", "gy", "gx")
-    return jax.shard_map(body, mesh=mesh, in_specs=in_specs, out_specs=out_specs, check_vma=False)
+    ny, nz = mesh.shape["gy"], mesh.shape["gz"]
+
+    def local(load_cases, density_level):
+        oz, oy, ox = density_level.shape
+        fits = mesh.shape["gx"] == load_cases.shape[0] == 2
+        fits = fits and ox == 128 and oz % 32 == 0 and oy % 8 == 0 and min(ny, nz) >= 3
+        if fits:
+            return split_cases(ny, nz, load_cases, density_level)
+        return body(load_cases, density_level)
+
+    return jax.shard_map(local, mesh=mesh, in_specs=in_specs, out_specs=out_specs, check_vma=False)

time: 221 us -> 48.3 us (0.22)
  local copies, waits for them, and re-layouts: 76.5 us -> 2.69 us
  blocking collectives: 50.4 us -> 0 us
  other arithmetic: 47.5 us -> 2.46 us
  Pallas kernels: 0 us -> 42.9 us
  starting transfers between devices: 28 us -> 0 us
  waiting for transfers between devices: 16.3 us -> 0 us
    all_gather x6 -> x0, blocking collectives: 50.4 us -> none  [joined(): values = lax.all_gather(values, axis, axis=dim, tiled=True)]
    reshape x8 -> x0, local copies, waits for them, and re-layouts: 45.5 us -> none  [the longest x4 38.1 us: restrict(): values.reshape(values.shape[0], values.shape[1] // 2, 2, values.shape[2]...]
    pallas_call x0 -> x1, Pallas kernels: none -> 42.9 us  [split_cases(): pl.pallas_call(lambda *refs: kernel(ny, nz, *refs), out_shape=jax.ShapeDt...]
    ppermute x12 -> x0, starting transfers between devices: 28 us -> none  [the longest x6 20.1 us: with_halo(): lax.ppermute(tail, axis, [(i, (i + 1) % count) for i in range(ends)])]
    reduce_sum x6 -> x0, other arithmetic: 19.7 us -> none  [restrict(): return values.reshape(values.shape[0], values.shape[1] // 2, 2, values.sh...]
    ppermute x12 -> x0, waiting for transfers between devices: 16.3 us -> none  [the longest x6 12.3 us: with_halo(): lax.ppermute(head, axis, [((i + 1) % count, i) for i in range(ends)])]
    add x46 -> x0, other arithmetic: 15.1 us -> none  [the longest x12 6.24 us: step(): return centre + weight * (scaled - mask * applied)]
    another operation x1 -> x0, local copies, waits for them, and re-layouts: 9.77 us -> none  [restrict(): values.reshape(values.shape[0], values.shape[1] // 2, 2, values.shape[2]...]
  transfers between devices with their start and end apart: 12 -> 0, of which waited for: 5 -> 0; matrix products, arithmetic and copies ran while one was open for 14% -> 0% of each run, Pallas kernels for 0% -> 0%
where the time goes in v1:
time: 48.3 us; the launch traced here: 48.1 us
  Pallas kernels  42.9 us (89%)
  local copies, waits for them, and re-layouts  2.69 us (6%)
  other arithmetic  2.46 us (5%)
    pallas_call x1, Pallas kernels, split_cases(): pl.pallas_call(lambda *refs: kernel(ny, nz, *refs), out_shape=jax.ShapeDt...  42.9 us
    transpose x1, local copies, waits for them, and re-layouts, split_cases(): return out.transpose(0, 2, 1, 3)  1.81 us
    div x1, other arithmetic, split_cases(): scaled = target * (1.0 / (14.0 * stiffness))  1 us

profile of v1, /device:TPU:0, one launch (start us, length us, event | category | flops | bytes accessed | tf_op | source)
XLA Modules:
  0.0 48.1 jit_solution(4966136778389121789)
XLA Ops:
  0.0 0.0 copy-start
  0.0 1.0 %multiply_divide_fusion = f32[8,32,128]{2,1,0:T(8,128)S(1)} fusion(s32[32,8,128]{2,1,0:T(8,128)} %param.3), kind=kLoop, calls=%fused_computation.8 | loop fusion | flops 262144 | bytes 262144 | tf_op jit(solution)/shard_map/div | solution.py:356
  1.0 0.0 copy-done
  1.0 0.0 copy-start.1
  1.0 0.8 %broadcast_multiply_fusion.refs_0_ = f32[2,8,32,128]{3,2,1,0:T(8,128)} fusion(f32[8,32,128]{2,1,0:T(8,128)S(1)} %multiply_divide_fusion, f32[2,32,8,128]{3,2,1,0:T(8,128)S(1)} %copy-done), kind=kLoop, calls=%fused_computation.7 | loop fusion | flops 65536 | bytes 655360 | tf_op jit(solution)/shard_map/mul | solution.py:356
  1.8 0.1 copy-done.1
  1.9 0.7 %fusion.2.refs_2_ = f32[8,32,128]{2,1,0:T(8,128)} fusion(s32[32,8,128]{2,1,0:T(8,128)S(1)} %copy-done.1), kind=kLoop, calls=%fused_computation.4 | loop fusion | flops 196608 | bytes 262144 | tf_op jit(solution)/shard_map/transpose | solution.py:354
  2.6 0.7 %copy.16 = f32[2,32,8,128]{3,1,2,0:T(8,128)} copy(f32[2,32,8,128]{3,2,1,0:T(8,128)S(1)} %copy-done) | data formatting | bytes 524288 | tf_op args[0]
  3.4 42.9 %shard_map.28 = f32[2,8,32,128]{3,2,1,0:T(8,128)} custom-call(f32[2,8,32,128]{3,2,1,0:T(8,128)} %broadcast_multiply_fusion.refs_0_, f32[2,8,32,128]{3,2,1,0:T(8,128)} %bitcast.11, f32[8,32,128]{2,1,0:T(8,128)} %fusion.2.refs_2_), custom_call_target="tpu_custom_call" | custom-call | tf_op jit(solution)/shard_map/pallas_call | solution.py:362
  46.3 1.8 %copy.5 = f32[2,32,8,128]{3,2,1,0:T(8,128)} copy(f32[2,32,8,128]{3,1,2,0:T(8,128)} %bitcast.10) | data formatting | bytes 524288 | tf_op jit(solution)/shard_map/transpose | solution.py:383
Async XLA Ops:
  0.0 1.0 %copy-start = (f32[2,32,8,128]{3,2,1,0:T(8,128)S(1)}, f32[2,32,8,128]{3,2,1,0:T(8,128)}, u32[]{:S(2)}) copy-start(f32[2,32,8,128]{3,2,1,0:T(8,128)} %param.2) | copy-start | bytes 786436
  1.0 0.9 %copy-start.1 = (s32[32,8,128]{2,1,0:T(8,128)S(1)}, s32[32,8,128]{2,1,0:T(8,128)}, u32[]{:S(2)}) copy-start(s32[32,8,128]{2,1,0:T(8,128)} %param.3) | copy-start | bytes 393220

commit v2 on v1

--- a/solution.py
+++ b/solution.py
@@ -140,11 +140,25 @@
     return step(guess_fine, prune(scaled_fine, 3, 0), second_weight, 1.0)
 
 
-HIGHEST = lax.Precision.HIGHEST
-
-
-def dot(a, b):
-    return jnp.dot(a, b, precision=HIGHEST, preferred_element_type=jnp.float32)
+def parts(a):
+    high = a.astype(jnp.bfloat16)
+    return high, (a - high.astype(jnp.float32)).astype(jnp.bfloat16)
+
+
+def product(a, b):
+    return jnp.dot(a, b, preferred_element_type=jnp.float32)
+
+
+def dot_right(a, matrix):
+    high, low = parts(a)
+    matrix = matrix.astype(jnp.bfloat16)
+    return product(high, matrix) + product(low, matrix)
+
+
+def dot_left(matrix, a):
+    high, low = parts(a)
+    matrix = matrix.astype(jnp.bfloat16)
+    return product(matrix, high) + product(matrix, low)
 
 
 def iota(shape, dim):
@@ -186,7 +200,7 @@
     pairs = (rows // 2) * depth
     across = pick(iota((length, length_out), 0) // 2 + first == iota((length, length_out), 1)) * 0.125
     along = pick(iota((pairs // 2, pairs), 1) // 2 == iota((pairs // 2, pairs), 0))
-    flat = dot(along, dot(values.reshape(pairs, length), across))
+    flat = dot_left(along, dot_right(values.reshape(pairs, length), across))
     return flat.reshape(rows // 2, depth // 2, length_out)
 
 
@@ -194,8 +208,8 @@
     rows, depth, length = values.shape
     across = pick(iota((length, length_out), 1) // 2 == iota((length, length_out), 0))
     along = pick(iota((depth_out, depth), 0) // 2 + offset == iota((depth_out, depth), 1))
-    wide = dot(values.reshape(rows * depth, length), across).reshape(rows, depth, length_out)
-    tall = [dot(along, wide[row]) for row in range(rows)]
+    wide = dot_right(values.reshape(rows * depth, length), across).reshape(rows, depth, length_out)
+    tall = [dot_left(along, wide[row]) for row in range(rows)]
     return jnp.stack([tall[row // 2] for row in range(2 * rows)], 0)
 
 
@@ -208,7 +222,7 @@
 SHIFTS = tuple((dy, dz) for dy in (-1, 0, 1) for dz in (-1, 0, 1))
 
 
-def kernel(ny, nz, g_ref, b_ref, s_ref, out_ref, gbuf, bbuf, sbuf, mbuf, lbuf, wide, obuf, rbuf,
+def kernel(ny, nz, g_ref, s_ref, out_ref, gbuf, sbuf, mbuf, lbuf, wide, obuf, rbuf,
            send_a, recv_a, send_b, recv_b, send_c, recv_c, send_d, recv_d):
     c, my, mz = lax.axis_index("gx"), lax.axis_index("gy"), lax.axis_index("gz")
     other = 1 - c
@@ -230,7 +244,6 @@
     for shift in SHIFTS:
         pl.semaphore_signal(barrier, 1, device_id=at(other, *near(*shift)), device_id_type=pl.DeviceIdType.MESH)
     gbuf[c, 3 : 3 + oy, 8 : 8 + oz, :] = g_ref[c]
-    bbuf[c] = b_ref[c]
     sbuf[c] = s_ref[...]
     pl.semaphore_wait(barrier, ny * nz - 1 + 9)
 
@@ -239,8 +252,19 @@
             src_ref=src, dst_ref=dst, send_sem=sends.at[slot], recv_sem=recvs.at[slot],
             device_id=device, device_id_type=pl.DeviceIdType.MESH,
         )
-        copy.start()
         return copy
+
+    def exists(dy, dz):
+        return (my + dy >= 0) & (my + dy < ny) & (mz + dz >= 0) & (mz + dz < nz)
+
+    def start_all(phase):
+        for copy, (dy, dz) in phase:
+            pl.when(exists(dy, dz))(copy.start)
+
+    def wait_all(phase):
+        for copy, (dy, dz) in phase:
+            pl.when(exists(dy, dz))(copy.wait_send)
+            pl.when(exists(-dy, -dz))(copy.wait_recv)
 
     def cut(shift, own, reach, room):
         if shift == 0:
@@ -255,28 +279,27 @@
                 continue
             fy, ty, ly = cut(dy, oy, 3, 3)
             fz, tz, lz = cut(dz, oz, 8, 8)
-            phase.append(remote(
+            phase.append((remote(
                 g_ref.at[who, fy : fy + ly, fz : fz + lz, :],
                 gbuf.at[c, ty : ty + ly, tz : tz + lz, :],
                 send_a, recv_a, slot, at(who, *near(dy, dz)),
-            ))
+            ), (dy, dz)))
             slot += 1
-    phase.append(remote(b_ref.at[other], bbuf.at[c], send_a, recv_a, slot, at(other, my, mz)))
-    phase.append(remote(s_ref, sbuf.at[c], send_a, recv_a, slot + 1, at(other, my, mz)))
-    for copy in phase:
-        copy.wait()
+    start_all(phase)
+    stiff_copy = remote(s_ref, sbuf.at[c], send_a, recv_a, slot, at(other, my, mz))
+    stiff_copy.start()
+    wait_all(phase)
 
     length = 2 * ox
     depth = oz + 16
-    fine = (depth, length, )
     def mask_fine(halo):
         return domain(oy + 2 * halo, depth, length, halo, 8, oy, oz, my, mz, ny, nz)
-    scaled = jnp.concatenate([gbuf[0], gbuf[1]], -1) * mask_fine(3)
-    target = jnp.concatenate([bbuf[0], bbuf[1]], -1)
-    stiff = jnp.concatenate([sbuf[0], sbuf[1]], -1)
+    scaled = jnp.where(mask_fine(3) > 0.0, jnp.concatenate([gbuf[0], gbuf[1]], -1), 0.0)
     guess = move(first_weight * scaled, scaled[1:-1], second_weight, mask_fine(2))
     applied = 16.0 * guess[2:-2] - 2.0 * blur(guess[1:-1])
-    rhs_mid = halve(target - stiff * applied[:, 8 : 8 + oz], ox)
+    stiff_copy.wait()
+    stiff = jnp.concatenate([sbuf[0], sbuf[1]], -1)
+    rhs_mid = halve(stiff * (14.0 * scaled[3:-3] - applied)[:, 8 : 8 + oz], ox)
     stiff_mid = halve(stiff, ox)
 
     hy, hz = oy // 2, oz // 2
@@ -285,18 +308,18 @@
     for slot, (dy, dz) in enumerate(shift for shift in SHIFTS if shift != (0, 0)):
         fy, ty, ly = cut(dy, hy, 4, 4)
         fz, tz, lz = cut(dz, hz, 8, 8)
-        phase.append(remote(
+        phase.append((remote(
             mbuf.at[4 + fy : 4 + fy + ly, 8 + fz : 8 + fz + lz, :],
             mbuf.at[ty : ty + ly, tz : tz + lz, :],
             send_b, recv_b, slot, at(c, *near(dy, dz)),
-        ))
+        ), (dy, dz)))
+    start_all(phase)
     packed_stiff = halve(stiff_mid, ox, ox // 2)
-    for copy in phase:
-        copy.wait()
+    wait_all(phase)
 
     def mask_mid(halo):
         return domain(hy + 2 * halo, hz + 16, ox, halo, 8, hy, hz, my, mz, ny, nz)
-    scaled_mid = mbuf[...] * mask_mid(4)
+    scaled_mid = jnp.where(mask_mid(4) > 0.0, mbuf[...], 0.0)
     guess_mid = move(first_weight * scaled_mid, scaled_mid[1:-1], second_weight, mask_mid(3))
     applied = 16.0 * guess_mid[3:-3] - 2.0 * blur(guess_mid[2:-2])
     residue = rhs_mid - stiff_mid * applied[:, 8 : 8 + hz] * 0.25
@@ -308,6 +331,8 @@
         phase.append(remote(
             lbuf.at[mz, my], lbuf.at[mz, my], send_c, recv_c, step - 1, at(c, *group(step))
         ))
+    for copy in phase:
+        copy.start()
     for copy in phase:
         copy.wait()
     packed = jnp.concatenate(
@@ -344,6 +369,7 @@
     obuf[0] = guess[:, :, :ox]
     obuf[1] = guess[:, :, ox:]
     copy = remote(obuf.at[other], rbuf, send_d, recv_d, 0, at(other, my, mz))
+    copy.start()
     out_ref[c] = obuf[c]
     copy.wait()
     out_ref[other] = rbuf[...]
@@ -352,8 +378,7 @@
 def split_cases(ny, nz, load_cases, density_level):
     stiffness = (0.05 + 0.95 * (density_level.astype(jnp.float32) / (LEVELS - 1)) ** 3)
     stiffness = stiffness.transpose(1, 0, 2)
-    target = load_cases.transpose(0, 2, 1, 3)
-    scaled = target * (1.0 / (14.0 * stiffness))
+    scaled = load_cases.transpose(0, 2, 1, 3) * (1.0 / (14.0 * stiffness))
     oy, oz, ox = stiffness.shape
     f32 = jnp.float32
     spec = pl.BlockSpec(memory_space=pltpu.VMEM)
@@ -361,25 +386,24 @@
     many = ny * nz - 1
     out = pl.pallas_call(
         lambda *refs: kernel(ny, nz, *refs),
-        out_shape=jax.ShapeDtypeStruct(target.shape, f32),
-        in_specs=[spec] * 3,
+        out_shape=jax.ShapeDtypeStruct(scaled.shape, f32),
+        in_specs=[spec] * 2,
         out_specs=spec,
         scratch_shapes=[
             pltpu.VMEM((2, oy + 6, oz + 16, ox), f32),
-            pltpu.VMEM((2, oy, oz, ox), f32),
             pltpu.VMEM((2, oy, oz, ox), f32),
             pltpu.VMEM((oy // 2 + 8, oz // 2 + 16, ox), f32),
             pltpu.VMEM((nz, ny, oy // 4, oz // 4, ox), f32),
             pltpu.VMEM((oy // 4 * ny + 4, oz // 4 * nz + 16, ox), f32),
             pltpu.VMEM((2, oy, oz, ox), f32),
             pltpu.VMEM((oy, oz, ox), f32),
-            dma((19,)), dma((19,)), dma((8,)), dma((8,)), dma((many,)), dma((many,)),
+            dma((18,)), dma((18,)), dma((8,)), dma((8,)), dma((many,)), dma((many,)),
             dma((1,)), dma((1,)),
         ],
         compiler_params=pltpu.CompilerParams(
             collective_id=0, has_side_effects=True, vmem_limit_bytes=60 * 2**20
         ),
-    )(scaled, target, stiffness)
+    )(scaled, stiffness)
     return out.transpose(0, 2, 1, 3)
 
 

time: 48.3 us -> 41 us (0.85)
  Pallas kernels: 42.9 us -> 36.3 us
  local copies, waits for them, and re-layouts: 2.69 us -> 1.96 us
    pallas_call x1, Pallas kernels: 42.9 us -> 36.3 us  [split_cases(): pl.pallas_call(lambda *refs: kernel(ny, nz, *refs), out_shape=jax.ShapeDt...]
    unnamed x5 -> x4, local copies, waits for them, and re-layouts: 0.89 us -> 0.15 us
where the time goes in v2:
time: 41 us; the launch traced here: 40.8 us
  Pallas kernels  36.3 us (89%)
  other arithmetic  2.46 us (6%)
  local copies, waits for them, and re-layouts  1.96 us (5%)
    pallas_call x1, Pallas kernels, split_cases(): pl.pallas_call(lambda *refs: kernel(ny, nz, *refs), out_shape=jax.ShapeDt...  36.3 us
    transpose x1, local copies, waits for them, and re-layouts, split_cases(): return out.transpose(0, 2, 1, 3)  1.81 us
    div x1, other arithmetic, split_cases(): scaled = load_cases.transpose(0, 2, 1, 3) * (1.0 / (14.0 * stiffness))  1 us

profile of v2, /device:TPU:0, one launch (start us, length us, event | category | flops | bytes accessed | tf_op | source)
XLA Modules:
  0.0 40.8 jit_solution(9646798829056928891)
XLA Ops:
  0.0 0.0 copy-start.1
  0.0 1.0 %multiply_divide_fusion = f32[8,32,128]{2,1,0:T(8,128)S(1)} fusion(s32[32,8,128]{2,1,0:T(8,128)} %param.3), kind=kLoop, calls=%fused_computation.7 | loop fusion | flops 262144 | bytes 262144 | tf_op jit(solution)/shard_map/div | solution.py:381
  1.0 0.0 copy-done.1
  1.0 0.0 copy-start
  1.0 0.8 %bitcast_multiply_fusion.refs_0_ = f32[2,8,32,128]{3,2,1,0:T(8,128)} fusion(f32[2,32,8,128]{3,2,1,0:T(8,128)S(1)} %copy-done.1, f32[8,32,128]{2,1,0:T(8,128)S(1)} %multiply_divide_fusion), kind=kLoop, calls=%fused_computation | loop fusion | flops 65536 | bytes 655360 | tf_op jit(solution)/shard_map/mul | solution.py:381
  1.8 0.1 copy-done
  1.9 0.7 %fusion.2.refs_1_ = f32[8,32,128]{2,1,0:T(8,128)} fusion(s32[32,8,128]{2,1,0:T(8,128)S(1)} %copy-done), kind=kLoop, calls=%fused_computation.4 | loop fusion | flops 196608 | bytes 262144 | tf_op jit(solution)/shard_map/transpose | solution.py:380
  2.6 36.3 %shard_map.28 = f32[2,8,32,128]{3,2,1,0:T(8,128)} custom-call(f32[2,8,32,128]{3,2,1,0:T(8,128)} %bitcast_multiply_fusion.refs_0_, f32[8,32,128]{2,1,0:T(8,128)} %fusion.2.refs_1_), custom_call_target="tpu_custom_call" | custom-call | tf_op jit(solution)/shard_map/pallas_call | solution.py:387
  39.0 1.8 %copy.5 = f32[2,32,8,128]{3,2,1,0:T(8,128)} copy(f32[2,32,8,128]{3,1,2,0:T(8,128)} %bitcast.7) | data formatting | bytes 524288 | tf_op jit(solution)/shard_map/transpose | solution.py:407
Async XLA Ops:
  0.0 1.0 %copy-start.1 = (f32[2,32,8,128]{3,2,1,0:T(8,128)S(1)}, f32[2,32,8,128]{3,2,1,0:T(8,128)}, u32[]{:S(2)}) copy-start(f32[2,32,8,128]{3,2,1,0:T(8,128)} %param.2) | copy-start | bytes 786436
  1.0 0.9 %copy-start = (s32[32,8,128]{2,1,0:T(8,128)S(1)}, s32[32,8,128]{2,1,0:T(8,128)}, u32[]{:S(2)}) copy-start(s32[32,8,128]{2,1,0:T(8,128)} %param.3) | copy-start | bytes 393220

commit v3 on v2

--- a/solution.py
+++ b/solution.py
@@ -364,14 +364,22 @@
     guess_mid = move(guess_mid, scaled_mid[3:-3], second_weight, mask_mid(1))
     guess = guess + double(guess_mid, depth, 4, length)
     guess = move(guess, scaled[2:-2], first_weight, mask_fine(1))
-    guess = move(guess, scaled[3:-3], second_weight, 1.0)[:, 8 : 8 + oz]
-
-    obuf[0] = guess[:, :, :ox]
-    obuf[1] = guess[:, :, ox:]
-    copy = remote(obuf.at[other], rbuf, send_d, recv_d, 0, at(other, my, mz))
-    copy.start()
+    phase = []
+    rows = oy // 4
+    for slot in range(4):
+        first, last = slot * rows, slot * rows + rows
+        piece = move(guess[first : last + 2], scaled[3 + first : 3 + last], second_weight, 1.0)
+        piece = piece[:, 8 : 8 + oz]
+        obuf[0, first:last] = piece[:, :, :ox]
+        obuf[1, first:last] = piece[:, :, ox:]
+        copy = remote(
+            obuf.at[other, first:last], rbuf.at[first:last], send_d, recv_d, slot, at(other, my, mz)
+        )
+        copy.start()
+        phase.append(copy)
     out_ref[c] = obuf[c]
-    copy.wait()
+    for copy in phase:
+        copy.wait()
     out_ref[other] = rbuf[...]
 
 
@@ -398,7 +406,7 @@
             pltpu.VMEM((2, oy, oz, ox), f32),
             pltpu.VMEM((oy, oz, ox), f32),
             dma((18,)), dma((18,)), dma((8,)), dma((8,)), dma((many,)), dma((many,)),
-            dma((1,)), dma((1,)),
+            dma((4,)), dma((4,)),
         ],
         compiler_params=pltpu.CompilerParams(
             collective_id=0, has_side_effects=True, vmem_limit_bytes=60 * 2**20

time: 41 us -> 40.9 us (level)
  no operation moved by 1% of the time
where the time goes in v3:
time: 40.9 us; the launch traced here: 40.7 us
  Pallas kernels  36.3 us (89%)
  other arithmetic  2.46 us (6%)
  local copies, waits for them, and re-layouts  1.96 us (5%)
    pallas_call x1, Pallas kernels, split_cases(): pl.pallas_call(lambda *refs: kernel(ny, nz, *refs), out_shape=jax.ShapeDt...  36.3 us
    transpose x1, local copies, waits for them, and re-layouts, split_cases(): return out.transpose(0, 2, 1, 3)  1.81 us
    div x1, other arithmetic, split_cases(): scaled = load_cases.transpose(0, 2, 1, 3) * (1.0 / (14.0 * stiffness))  1 us

profile of v3, /device:TPU:0, one launch (start us, length us, event | category | flops | bytes accessed | tf_op | source)
XLA Modules:
  0.0 40.7 jit_solution(12796265438569099242)
XLA Ops:
  0.0 0.0 copy-start.1
  0.0 1.0 %multiply_divide_fusion = f32[8,32,128]{2,1,0:T(8,128)S(1)} fusion(s32[32,8,128]{2,1,0:T(8,128)} %param.3), kind=kLoop, calls=%fused_computation.7 | loop fusion | flops 262144 | bytes 262144 | tf_op jit(solution)/shard_map/div | solution.py:389
  1.0 0.0 copy-done.1
  1.0 0.0 copy-start
  1.0 0.8 %bitcast_multiply_fusion.refs_0_ = f32[2,8,32,128]{3,2,1,0:T(8,128)} fusion(f32[2,32,8,128]{3,2,1,0:T(8,128)S(1)} %copy-done.1, f32[8,32,128]{2,1,0:T(8,128)S(1)} %multiply_divide_fusion), kind=kLoop, calls=%fused_computation | loop fusion | flops 65536 | bytes 655360 | tf_op jit(solution)/shard_map/mul | solution.py:389
  1.8 0.1 copy-done
  1.9 0.7 %fusion.2.refs_1_ = f32[8,32,128]{2,1,0:T(8,128)} fusion(s32[32,8,128]{2,1,0:T(8,128)S(1)} %copy-done), kind=kLoop, calls=%fused_computation.4 | loop fusion | flops 196608 | bytes 262144 | tf_op jit(solution)/shard_map/transpose | solution.py:388
  2.6 36.3 %shard_map.28 = f32[2,8,32,128]{3,2,1,0:T(8,128)} custom-call(f32[2,8,32,128]{3,2,1,0:T(8,128)} %bitcast_multiply_fusion.refs_0_, f32[8,32,128]{2,1,0:T(8,128)} %fusion.2.refs_1_), custom_call_target="tpu_custom_call" | custom-call | tf_op jit(solution)/shard_map/pallas_call | solution.py:395
  38.9 1.8 %copy.5 = f32[2,32,8,128]{3,2,1,0:T(8,128)} copy(f32[2,32,8,128]{3,1,2,0:T(8,128)} %bitcast.7) | data formatting | bytes 524288 | tf_op jit(solution)/shard_map/transpose | solution.py:415
Async XLA Ops:
  0.0 1.0 %copy-start.1 = (f32[2,32,8,128]{3,2,1,0:T(8,128)S(1)}, f32[2,32,8,128]{3,2,1,0:T(8,128)}, u32[]{:S(2)}) copy-start(f32[2,32,8,128]{3,2,1,0:T(8,128)} %param.2) | copy-start | bytes 786436
  1.0 0.9 %copy-start = (s32[32,8,128]{2,1,0:T(8,128)S(1)}, s32[32,8,128]{2,1,0:T(8,128)}, u32[]{:S(2)}) copy-start(s32[32,8,128]{2,1,0:T(8,128)} %param.3) | copy-start | bytes 393220
